TPU v7x, 32 devices: a whole 2x2x4 slice. The times are simulated.
32 devices in a mesh: groups: 2 (over y), tmpl: 4 (over z), sta: 2 (over x), comp: 2 (over core).
Axes of the slice: x: 2, y: 2, z: 4, core: 2. Of those that a mesh axis runs over, the one named last changes fastest.
Arguments:
- templates: bfloat16 [1024, 32, 3, 256], P(('groups', 'tmpl'), ('sta', 'comp')), parts along dimension 0, may hold values from -6 to 6
- data: bfloat16 [64, 3, 2048], P(('groups', 'sta', 'comp'), None, 'tmpl'), parts along dimension 0, may hold values from -21 to 21
- tail: bfloat16 [64, 3, 512], P(('groups', 'sta', 'comp')), parts along dimension 0, may hold values from -21 to 21
- offsets: int32 [64], P(('groups', 'sta', 'comp')), parts along dimension 0, may hold values from 0 to 255, as said below
- weights: int32 [64], P(('groups', 'sta', 'comp')), parts along dimension 0, may hold values from 1 to 4
- mask: int32 [1024, 32], P(('groups', 'tmpl'), ('sta', 'comp')), parts along dimension 0, may hold values 0 or 1
Outputs:
- stack: float32 [1024, 2048], P(('groups', 'tmpl'), ('sta', 'comp')), parts along dimension 0
There are 2 independent parts, one for each index of `groups`. A program takes and returns all parts, laid end to end along the dimension named above; each array names one. Nothing has to cross between parts.
Inputs may be any that keep to these rules, and one draw needn't show every extreme that they name: `offsets`: some station's offset is 0 and some station's is 255.
All inputs are finite; a program needn't handle non-finite values. No bound on the sum of `mask` on one device may be relied on, other than what follows from the above.
Results may differ from a plain program's by a relative error of at most 0.0055.
Values may be sent and summed in bfloat16 or wider, within the bound.
No kernel may reach another device: no remote copies, remote signals or barrier semaphores. Data moves between devices by JAX's collectives and lax.ppermute only.
A program may use at most 192 MiB of HBM per device.

v0:
```python
import jax
import jax.numpy as jnp
from jax import lax
from jax.sharding import PartitionSpec as P

EPS = 1e-05


def passed_along(x, axis, by):
    devices = lax.axis_size(axis)
    pairs = [(i, i + by) for i in range(devices) if 0 <= i + by < devices]
    return lax.ppermute(x, axis, pairs)


def unit_templates(templates):
    values = templates.astype(jnp.float32)
    centred = values - jnp.mean(values, axis=-1, keepdims=True)
    spread = jnp.mean(centred * centred, axis=-1, keepdims=True)
    return (centred * lax.rsqrt(spread + EPS)).astype(jnp.bfloat16)


def lag_table(rows, length, span):
    lead = rows.shape[:-1]
    padded = jnp.concatenate([rows, jnp.zeros(lead + (1,), rows.dtype)], axis=-1)
    period = padded.shape[-1]
    tiled = jnp.tile(padded, (1,) * len(lead) + (length + 1,))
    cut = tiled[..., : length * (period + 1)]
    return cut.reshape(lead + (length, period + 1))[..., :span]


def table_factor(table, length):
    values = table.astype(jnp.float32)
    middle = jnp.sum(values, axis=-2) / length
    squares = jnp.sum(values * values, axis=-2) / length
    spread = squares - middle * middle
    return 1.0 / (length * jnp.sqrt(spread + EPS))


def shards(templates, data, tail, offsets, weights, mask):
    length = templates.shape[-1]
    stations = data.shape[0]
    span = data.shape[-1]
    count = templates.shape[0]
    owners = lax.axis_size("tmpl")
    received = passed_along(data, "tmpl", -1)
    closing = lax.axis_index("tmpl") == owners - 1
    extended = jnp.concatenate([data, jnp.where(closing, tail, received)], axis=2)
    units = unit_templates(templates)
    station_units = jnp.transpose(units, (1, 0, 2, 3))
    station_weight = jnp.transpose(mask.astype(jnp.float32) * weights.astype(jnp.float32)[None, :])
    reach = span + length - 1
    width_sent = extended.shape[-1]
    records = lax.all_gather(extended, "tmpl", axis=2, tiled=True)
    parts = records.shape[-1] // width_sent
    grouped = records.reshape(stations, 3, parts, width_sent)

    def add_station(carry, inputs):
        unit_rows, window_rows, begin, column = inputs
        window = lax.dynamic_slice_in_dim(window_rows, begin, reach, 2)
        table = lag_table(window, length, span)
        factor_rows = table_factor(table, length)
        products = jnp.einsum(
            "tck,cpkj->tcpj", unit_rows, table, preferred_element_type=jnp.float32
        )
        scaled = jnp.sum(products * factor_rows[None], axis=1)
        return (carry + column[:, None, None] * scaled, None)

    start_rows = jnp.zeros((count, parts, span), jnp.float32)
    stacked, _ = lax.scan(
        add_station, start_rows, (station_units, grouped, offsets, station_weight)
    )
    stacked = stacked.reshape(count, parts * span)
    return lax.psum_scatter(stacked, ("sta", "comp"), scatter_dimension=1, tiled=True)


def solution(mesh):
    in_specs = (
        P(("groups", "tmpl"), ("sta", "comp"), None, None),
        P(("groups", "sta", "comp"), None, "tmpl"),
        P(("groups", "sta", "comp"), None, None),
        P(("groups", "sta", "comp")),
        P(("groups", "sta", "comp")),
        P(("groups", "tmpl"), ("sta", "comp")),
    )
    out_specs = P(("groups", "tmpl"), ("sta", "comp"))
    return jax.shard_map(shards, mesh=mesh, in_specs=in_specs, out_specs=out_specs, check_vma=False)
```

profile of v0, /device:TPU:0, one launch (start us, length us, event | category | flops | bytes accessed | tf_op | source)
XLA Modules:
  0.0 428.5 jit_solution(4442578683296231122)
XLA Ops:
  14.3 16.3 %all_gather.3 = bf16[8,3,4096]{2,0,1:T(8,128)(2,1)S(1)} all-gather(bf16[8,3,1024]{2,0,1:T(8,128)(2,1)S(1)} %pad_maximum_fusion), channel_id=1, replica_groups=mesh['groups'=2,'tmpl'=4,'sta'=2,'comp'=2] {'tmpl'}, dimensions={2}, use_global_device_ids=true | all-gather | bytes 245760 | tf_op jit(solution)/shard_map/all_gather | solution.py:53
  30.8 361.8 %while.14 = (s32[]{:T(128)}, f32[128,4,512]{0,2,1:T(8,128)}, f32[8,128]{1,0:T(8,128)S(1)}, s32[8]{0:T(128)S(1)}, bf16[8,3,4,1024]{3,2,0,1:T(4,128)(2,1)S(1)}, /*...) while((s32[]{:T(128)}, f32[128,4,512]{0,2,1:T(8,128)}, ...), condition=%wide.region_6.7_spmd.clone, body=%wide.region_2.6_spmd.clone.sunk | while | flops 411072512 | bytes 68151520 | solution.py:69
  35.9 6.8 %tile.18 = bf16[3,4,197376]{2,1,0:T(4,128)(2,1)} reshape(bf16[3,4,257,768]{3,2,1,0:T(8,128)(2,1)} %tile.17) | data formatting | bytes 9474048 | tf_op jit(solution)/shard_map/while/body/eval_jaxpr/tile | solution.py:26
  42.7 6.9 %slice.24 = bf16[3,4,196864]{2,1,0:T(4,128)(2,1)} slice(bf16[3,4,197376]{2,1,0:T(4,128)(2,1)} %tile.18), slice={[0:3], [0:4], [0:196864]} | slice | bytes 9449472 | tf_op jit(solution)/shard_map/while/body/eval_jaxpr/slice | solution.py:27
  49.6 12.9 %reshape.56 = bf16[3,4,256,769]{3,2,1,0:T(8,128)(2,1)} reshape(bf16[3,4,196864]{2,1,0:T(4,128)(2,1)} %slice.24) | data formatting | bytes 9449472 | tf_op jit(solution)/shard_map/while/body/eval_jaxpr/reshape | solution.py:28
  64.4 2.8 copy.24
  67.2 3.6 fusion.17
  70.9 3.8 multiply_reduce_fusion.2
  81.1 6.8 %tile.18 = bf16[3,4,197376]{2,1,0:T(4,128)(2,1)} reshape(bf16[3,4,257,768]{3,2,1,0:T(8,128)(2,1)} %tile.17) | data formatting | bytes 9474048 | tf_op jit(solution)/shard_map/while/body/eval_jaxpr/tile | solution.py:26
  87.9 6.9 %slice.24 = bf16[3,4,196864]{2,1,0:T(4,128)(2,1)} slice(bf16[3,4,197376]{2,1,0:T(4,128)(2,1)} %tile.18), slice={[0:3], [0:4], [0:196864]} | slice | bytes 9449472 | tf_op jit(solution)/shard_map/while/body/eval_jaxpr/slice | solution.py:27
  94.8 12.9 %reshape.56 = bf16[3,4,256,769]{3,2,1,0:T(8,128)(2,1)} reshape(bf16[3,4,196864]{2,1,0:T(4,128)(2,1)} %slice.24) | data formatting | bytes 9449472 | tf_op jit(solution)/shard_map/while/body/eval_jaxpr/reshape | solution.py:28
  109.6 2.8 copy.24
  112.4 3.6 fusion.17
  116.1 3.8 multiply_reduce_fusion.2
  126.3 6.8 %tile.18 = bf16[3,4,197376]{2,1,0:T(4,128)(2,1)} reshape(bf16[3,4,257,768]{3,2,1,0:T(8,128)(2,1)} %tile.17) | data formatting | bytes 9474048 | tf_op jit(solution)/shard_map/while/body/eval_jaxpr/tile | solution.py:26
  133.1 6.9 %slice.24 = bf16[3,4,196864]{2,1,0:T(4,128)(2,1)} slice(bf16[3,4,197376]{2,1,0:T(4,128)(2,1)} %tile.18), slice={[0:3], [0:4], [0:196864]} | slice | bytes 9449472 | tf_op jit(solution)/shard_map/while/body/eval_jaxpr/slice | solution.py:27
  140.1 12.9 %reshape.56 = bf16[3,4,256,769]{3,2,1,0:T(8,128)(2,1)} reshape(bf16[3,4,196864]{2,1,0:T(4,128)(2,1)} %slice.24) | data formatting | bytes 9449472 | tf_op jit(solution)/shard_map/while/body/eval_jaxpr/reshape | solution.py:28
  154.8 2.8 copy.24
  157.7 3.6 fusion.17
  161.3 3.8 multiply_reduce_fusion.2
  171.6 6.8 %tile.18 = bf16[3,4,197376]{2,1,0:T(4,128)(2,1)} reshape(bf16[3,4,257,768]{3,2,1,0:T(8,128)(2,1)} %tile.17) | data formatting | bytes 9474048 | tf_op jit(solution)/shard_map/while/body/eval_jaxpr/tile | solution.py:26
  178.4 6.9 %slice.24 = bf16[3,4,196864]{2,1,0:T(4,128)(2,1)} slice(bf16[3,4,197376]{2,1,0:T(4,128)(2,1)} %tile.18), slice={[0:3], [0:4], [0:196864]} | slice | bytes 9449472 | tf_op jit(solution)/shard_map/while/body/eval_jaxpr/slice | solution.py:27
  185.3 12.9 %reshape.56 = bf16[3,4,256,769]{3,2,1,0:T(8,128)(2,1)} reshape(bf16[3,4,196864]{2,1,0:T(4,128)(2,1)} %slice.24) | data formatting | bytes 9449472 | tf_op jit(solution)/shard_map/while/body/eval_jaxpr/reshape | solution.py:28
  200.0 2.8 copy.24
  202.9 3.6 fusion.17
  206.5 3.8 multiply_reduce_fusion.2
  216.8 6.8 %tile.18 = bf16[3,4,197376]{2,1,0:T(4,128)(2,1)} reshape(bf16[3,4,257,768]{3,2,1,0:T(8,128)(2,1)} %tile.17) | data formatting | bytes 9474048 | tf_op jit(solution)/shard_map/while/body/eval_jaxpr/tile | solution.py:26
  223.6 6.9 %slice.24 = bf16[3,4,196864]{2,1,0:T(4,128)(2,1)} slice(bf16[3,4,197376]{2,1,0:T(4,128)(2,1)} %tile.18), slice={[0:3], [0:4], [0:196864]} | slice | bytes 9449472 | tf_op jit(solution)/shard_map/while/body/eval_jaxpr/slice | solution.py:27
  230.5 12.9 %reshape.56 = bf16[3,4,256,769]{3,2,1,0:T(8,128)(2,1)} reshape(bf16[3,4,196864]{2,1,0:T(4,128)(2,1)} %slice.24) | data formatting | bytes 9449472 | tf_op jit(solution)/shard_map/while/body/eval_jaxpr/reshape | solution.py:28
  245.3 2.8 copy.24
  248.1 3.6 fusion.17
  251.7 3.8 multiply_reduce_fusion.2
  262.0 6.8 %tile.18 = bf16[3,4,197376]{2,1,0:T(4,128)(2,1)} reshape(bf16[3,4,257,768]{3,2,1,0:T(8,128)(2,1)} %tile.17) | data formatting | bytes 9474048 | tf_op jit(solution)/shard_map/while/body/eval_jaxpr/tile | solution.py:26
  268.8 6.9 %slice.24 = bf16[3,4,196864]{2,1,0:T(4,128)(2,1)} slice(bf16[3,4,197376]{2,1,0:T(4,128)(2,1)} %tile.18), slice={[0:3], [0:4], [0:196864]} | slice | bytes 9449472 | tf_op jit(solution)/shard_map/while/body/eval_jaxpr/slice | solution.py:27
  275.7 12.9 %reshape.56 = bf16[3,4,256,769]{3,2,1,0:T(8,128)(2,1)} reshape(bf16[3,4,196864]{2,1,0:T(4,128)(2,1)} %slice.24) | data formatting | bytes 9449472 | tf_op jit(solution)/shard_map/while/body/eval_jaxpr/reshape | solution.py:28
  293.3 3.6 fusion.17
  297.0 3.8 multiply_reduce_fusion.2
  307.2 6.8 %tile.18 = bf16[3,4,197376]{2,1,0:T(4,128)(2,1)} reshape(bf16[3,4,257,768]{3,2,1,0:T(8,128)(2,1)} %tile.17) | data formatting | bytes 9474048 | tf_op jit(solution)/shard_map/while/body/eval_jaxpr/tile | solution.py:26
  314.0 6.9 %slice.24 = bf16[3,4,196864]{2,1,0:T(4,128)(2,1)} slice(bf16[3,4,197376]{2,1,0:T(4,128)(2,1)} %tile.18), slice={[0:3], [0:4], [0:196864]} | slice | bytes 9449472 | tf_op jit(solution)/shard_map/while/body/eval_jaxpr/slice | solution.py:27
  320.9 12.9 %reshape.56 = bf16[3,4,256,769]{3,2,1,0:T(8,128)(2,1)} reshape(bf16[3,4,196864]{2,1,0:T(4,128)(2,1)} %slice.24) | data formatting | bytes 9449472 | tf_op jit(solution)/shard_map/while/body/eval_jaxpr/reshape | solution.py:28
  338.5 3.6 fusion.17
  342.2 3.8 multiply_reduce_fusion.2
  352.4 6.8 %tile.18 = bf16[3,4,197376]{2,1,0:T(4,128)(2,1)} reshape(bf16[3,4,257,768]{3,2,1,0:T(8,128)(2,1)} %tile.17) | data formatting | bytes 9474048 | tf_op jit(solution)/shard_map/while/body/eval_jaxpr/tile | solution.py:26
  359.2 6.9 %slice.24 = bf16[3,4,196864]{2,1,0:T(4,128)(2,1)} slice(bf16[3,4,197376]{2,1,0:T(4,128)(2,1)} %tile.18), slice={[0:3], [0:4], [0:196864]} | slice | bytes 9449472 | tf_op jit(solution)/shard_map/while/body/eval_jaxpr/slice | solution.py:27
  366.1 12.9 %reshape.56 = bf16[3,4,256,769]{3,2,1,0:T(8,128)(2,1)} reshape(bf16[3,4,196864]{2,1,0:T(4,128)(2,1)} %slice.24) | data formatting | bytes 9449472 | tf_op jit(solution)/shard_map/while/body/eval_jaxpr/reshape | solution.py:28
  383.7 3.6 fusion.17
  387.4 3.8 multiply_reduce_fusion.2
  395.2 26.5 %reduce-scatter.2.cloned.1.call-done = f32[128,512]{1,0:T(8,128)} async-done(((f32[128,2048]{1,0:T(8,128)}), f32[128,512]{1,0:T(8,128)}) %reduce-scatter.2.cloned.1.call-update) | async-done | bytes 262160 | tf_op jit(solution)/shard_map/reduce_scatter | solution.py:73
  (135 shorter events, 70.9 us)
Async XLA Ops:
  6.5 7.7 %copy-start.4 = (bf16[8,3,512]{2,0,1:T(8,128)(2,1)S(1)}, bf16[8,3,512]{2,0,1:T(8,128)(2,1)}, u32[]{:S(2)}) copy-start(bf16[8,3,512]{2,0,1:T(8,128)(2,1)} %param.9) | copy-start | bytes 73732
  6.5 5.8 %copy-start.2 = (bf16[128,8,3,256]{3,1,2,0:T(8,128)(2,1)S(1)}, bf16[128,8,3,256]{3,1,2,0:T(8,128)(2,1)}, u32[]{:S(2)}) copy-start(bf16[128,8,3,256]{3,1,2,0:T(8,128)(2,1)} %param.8) | copy-start | bytes 4718596
  6.5 7.6 %copy-start.6 = (s32[8]{0:T(128)S(1)}, s32[8]{0:T(128)}, u32[]{:S(2)}) copy-start(s32[8]{0:T(128)} %param.12) | copy-start | bytes 100
  6.5 7.6 %copy-start.5 = (s32[128,8]{0,1:T(8,128)S(1)}, s32[128,8]{0,1:T(8,128)}, u32[]{:S(2)}) copy-start(s32[128,8]{0,1:T(8,128)} %param.13) | copy-start | bytes 12292
  6.5 7.7 %copy-start.3 = (bf16[8,3,512]{2,0,1:T(8,128)(2,1)S(1)}, bf16[8,3,512]{2,0,1:T(8,128)(2,1)}, u32[]{:S(2)}) copy-start(bf16[8,3,512]{2,0,1:T(8,128)(2,1)} %param.10) | copy-start | bytes 73732
  6.5 415.1 %reduce-scatter.2.cloned.1.call-start = ((), (), s32[]{:S(2)}) async-start(), calls=%async_computation.1 | async-start | bytes 1310720 | tf_op jit(solution)/shard_map/reduce_scatter | solution.py:73
  6.6 7.7 %collective-permute-start = (bf16[8,3,512]{2,0,1:T(8,128)(2,1)}, bf16[8,3,512]{2,0,1:T(8,128)(2,1)S(1)}, u32[]{:S(2)}, u32[]{:S(2)}) collective-permute-start(bf16[8,3,512]{2,0,1:T(8,128)(2,1)} %param.9), channel_id=1, source_target_pairs={{4,0},{8,4},{12,8},{5,1},{9,5},{13,9},{6,2},{10,6},{14,10},{7,3},{... | collective-permute-start | bytes 73736 | tf_op jit(solution)/shard_map/ppermute | solution.py:12
  9.9 20.9 %copy-start.7 = (s32[8]{0:T(128)S(1)}, s32[8]{0:T(128)}, u32[]{:S(2)}) copy-start(s32[8]{0:T(128)} %param.11) | copy-start | bytes 100
  62.5 1.9 slice-start
  70.9 3.8 copy-start
  75.0 1.0 copy-start.1
  107.7 1.9 slice-start
  116.1 3.8 copy-start
  120.3 1.0 copy-start.1
  152.9 1.9 slice-start
  161.3 3.8 copy-start
  165.5 1.0 copy-start.1
  198.1 1.9 slice-start
  206.5 3.8 copy-start
  210.7 1.0 copy-start.1
  243.4 1.9 slice-start
  251.7 3.8 copy-start
  255.9 1.0 copy-start.1
  288.6 1.9 slice-start
  297.0 3.8 copy-start
  301.1 1.0 copy-start.1
  333.8 1.9 slice-start
  342.2 3.8 copy-start
  346.3 1.0 copy-start.1
  379.0 1.9 slice-start
  387.4 3.8 copy-start
  391.6 1.0 copy-start.1
Sparse Core Ops, SparseCore 0:
  395.3 26.3 reduce-scatter.1
where the time goes:
time: 431 us; the launch traced here: 428 us
  local copies, waits for them, and re-layouts  287 us (67%)
  other arithmetic  38.1 us (9%)
  matrix products  30 us (7%)
  waiting for transfers between devices  26.5 us (6%)
  blocking collectives  16.3 us (4%)
  loops' own time  15.6 us (4%)
  between operations  13.5 us (3%)
    reshape x8, local copies, waits for them, and re-layouts, lag_table(): return cut.reshape(lead + (length, period + 1))[..., :span]  103 us
    another operation x16, local copies, waits for them, and re-layouts, lag_table(): tiled = jnp.tile(padded, (1,) * len(lead) + (length + 1,))  74.7 us
    slice x8, local copies, waits for them, and re-layouts, lag_table(): cut = tiled[..., :length * (period + 1)]  55.2 us
    while x56, local copies, waits for them, and re-layouts  45.7 us
    dot_general x8, matrix products, add_station(): jnp.einsum('tck,cpkj->tcpj', unit_rows, table, preferred_element_type=jnp...  30 us
    reduce_sum x8, other arithmetic, table_factor(): squares = jnp.sum(values * values, axis=-2) / length  28.8 us
    reduce_scatter x1, waiting for transfers between devices, shards(): lax.psum_scatter(stacked, ('sta', 'comp'), scatter_dimension=1, tiled=True)  26.5 us
    all_gather x1, blocking collectives, shards(): records = lax.all_gather(extended, 'tmpl', axis=2, tiled=True)  16.3 us
  transfers between devices with their start and end apart: 2, of which 1 were waited for; matrix products, arithmetic and copies ran while one was open for 1% of the time, Pallas kernels for 0%

commit v1 on v0

--- a/solution.py
+++ b/solution.py
@@ -50,7 +50,12 @@
     station_weight = jnp.transpose(mask.astype(jnp.float32) * weights.astype(jnp.float32)[None, :])
     reach = span + length - 1
     width_sent = extended.shape[-1]
-    records = lax.all_gather(extended, "tmpl", axis=2, tiled=True)
+    ring = [extended]
+    for hop in range(3):
+        ring.append(lax.ppermute(ring[-1], "tmpl", [(dev, (dev + 1) % 4) for dev in range(4)]))
+    records = jnp.roll(
+        jnp.concatenate(ring[::-1], axis=2), (lax.axis_index("tmpl") + 1) * ring[0].shape[2], axis=2
+    )
     parts = records.shape[-1] // width_sent
     grouped = records.reshape(stations, 3, parts, width_sent)
 

time: 431 us -> 428 us (level)
  blocking collectives: 16.3 us -> 0 us
  waiting for transfers between devices: 26.5 us -> 39 us
    all_gather x1 -> x0, blocking collectives: 16.3 us -> none  [shards(): records = lax.all_gather(extended, 'tmpl', axis=2, tiled=True)]
    ppermute x0 -> x3, waiting for transfers between devices: none -> 14.3 us  [shards(): lax.ppermute(ring[-1], 'tmpl', [(dev, (dev + 1) % 4) for dev in range(4)])]
  transfers between devices with their start and end apart: 2 -> 5, of which waited for: 1 -> 5; matrix products, arithmetic and copies ran while one was open for 1% -> 1% of each run, Pallas kernels for 0% -> 0%
where the time goes in v1:
time: 428 us; the launch traced here: 425 us
  local copies, waits for them, and re-layouts  287 us (67%)
  waiting for transfers between devices  39 us (9%)
  other arithmetic  38.1 us (9%)
  matrix products  30 us (7%)
  loops' own time  14.2 us (3%)
  between operations  13.6 us (3%)
    reshape x8, local copies, waits for them, and re-layouts, lag_table(): return cut.reshape(lead + (length, period + 1))[..., :span]  103 us
    another operation x16, local copies, waits for them, and re-layouts, lag_table(): tiled = jnp.tile(padded, (1,) * len(lead) + (length + 1,))  74.5 us
    slice x8, local copies, waits for them, and re-layouts, lag_table(): cut = tiled[..., :length * (period + 1)]  55.4 us
    while x56, local copies, waits for them, and re-layouts  45.5 us
    dot_general x8, matrix products, add_station(): jnp.einsum('tck,cpkj->tcpj', unit_rows, table, preferred_element_type=jnp...  30 us
    reduce_sum x8, other arithmetic, table_factor(): squares = jnp.sum(values * values, axis=-2) / length  28.8 us
    reduce_scatter x1, waiting for transfers between devices, shards(): lax.psum_scatter(stacked, ('sta', 'comp'), scatter_dimension=1, tiled=True)  23.3 us
    ppermute x3, waiting for transfers between devices, shards(): lax.ppermute(ring[-1], 'tmpl', [(dev, (dev + 1) % 4) for dev in range(4)])  14.3 us
  transfers between devices with their start and end apart: 5, of which 5 were waited for; matrix products, arithmetic and copies ran while one was open for 1% of the time, Pallas kernels for 0%

profile of v1, /device:TPU:0, one launch (start us, length us, event | category | flops | bytes accessed | tf_op | source)
XLA Modules:
  0.0 425.4 jit_solution(8595415393258071333)
XLA Ops:
  16.1 4.5 %collective-permute-done.1 = bf16[8,3,1024]{2,0,1:T(8,128)(2,1)S(1)} collective-permute-done((bf16[8,3,1024]{2,0,1:T(8,128)(2,1)S(1)}, bf16[8,3,1024]{2,0,1:T(8,128)(2,1)S(1)}, u32[]{:S(2)}, u32[]{:S(2)}) %collective-permute-start.1) | collective-permute-done | bytes 49184 | tf_op jit(solution)/shard_map/ppermute | solution.py:55
  22.4 4.0 collective-permute-done.2
  26.5 5.8 %collective-permute-done.3 = bf16[8,3,1024]{2,0,1:T(8,128)(2,1)S(1)} collective-permute-done((bf16[8,3,1024]{2,0,1:T(8,128)(2,1)S(1)}, bf16[8,3,1024]{2,0,1:T(8,128)(2,1)S(1)}, u32[]{:S(2)}, u32[]{:S(2)}) %collective-permute-start.3) | collective-permute-done | bytes 49184 | tf_op jit(solution)/shard_map/ppermute | solution.py:55
  32.6 360.0 %while.14 = (s32[]{:T(128)}, f32[128,4,512]{0,2,1:T(8,128)}, f32[8,128]{1,0:T(8,128)S(1)}, s32[8]{0:T(128)S(1)}, bf16[8,3,4,1024]{3,2,0,1:T(4,128)(2,1)S(1)}, /*...) while((s32[]{:T(128)}, f32[128,4,512]{0,2,1:T(8,128)}, ...), condition=%wide.region_6.7_spmd.clone, body=%wide.region_2.6_spmd.clone.sunk | while | flops 411072512 | bytes 68151520 | solution.py:74
  37.6 6.8 %tile.18 = bf16[3,4,197376]{2,1,0:T(4,128)(2,1)} reshape(bf16[3,4,257,768]{3,2,1,0:T(8,128)(2,1)} %tile.17) | data formatting | bytes 9474048 | tf_op jit(solution)/shard_map/while/body/eval_jaxpr/tile | solution.py:26
  44.4 6.9 %slice.24 = bf16[3,4,196864]{2,1,0:T(4,128)(2,1)} slice(bf16[3,4,197376]{2,1,0:T(4,128)(2,1)} %tile.18), slice={[0:3], [0:4], [0:196864]} | slice | bytes 9449472 | tf_op jit(solution)/shard_map/while/body/eval_jaxpr/slice | solution.py:27
  51.3 12.9 %reshape.56 = bf16[3,4,256,769]{3,2,1,0:T(8,128)(2,1)} reshape(bf16[3,4,196864]{2,1,0:T(4,128)(2,1)} %slice.24) | data formatting | bytes 9449472 | tf_op jit(solution)/shard_map/while/body/eval_jaxpr/reshape | solution.py:28
  68.9 3.6 fusion.17
  72.5 3.8 multiply_reduce_fusion.2
  82.6 6.8 %tile.18 = bf16[3,4,197376]{2,1,0:T(4,128)(2,1)} reshape(bf16[3,4,257,768]{3,2,1,0:T(8,128)(2,1)} %tile.17) | data formatting | bytes 9474048 | tf_op jit(solution)/shard_map/while/body/eval_jaxpr/tile | solution.py:26
  89.4 6.9 %slice.24 = bf16[3,4,196864]{2,1,0:T(4,128)(2,1)} slice(bf16[3,4,197376]{2,1,0:T(4,128)(2,1)} %tile.18), slice={[0:3], [0:4], [0:196864]} | slice | bytes 9449472 | tf_op jit(solution)/shard_map/while/body/eval_jaxpr/slice | solution.py:27
  96.3 12.9 %reshape.56 = bf16[3,4,256,769]{3,2,1,0:T(8,128)(2,1)} reshape(bf16[3,4,196864]{2,1,0:T(4,128)(2,1)} %slice.24) | data formatting | bytes 9449472 | tf_op jit(solution)/shard_map/while/body/eval_jaxpr/reshape | solution.py:28
  113.9 3.6 fusion.17
  117.5 3.8 multiply_reduce_fusion.2
  127.6 6.8 %tile.18 = bf16[3,4,197376]{2,1,0:T(4,128)(2,1)} reshape(bf16[3,4,257,768]{3,2,1,0:T(8,128)(2,1)} %tile.17) | data formatting | bytes 9474048 | tf_op jit(solution)/shard_map/while/body/eval_jaxpr/tile | solution.py:26
  134.4 6.9 %slice.24 = bf16[3,4,196864]{2,1,0:T(4,128)(2,1)} slice(bf16[3,4,197376]{2,1,0:T(4,128)(2,1)} %tile.18), slice={[0:3], [0:4], [0:196864]} | slice | bytes 9449472 | tf_op jit(solution)/shard_map/while/body/eval_jaxpr/slice | solution.py:27
  141.3 12.9 %reshape.56 = bf16[3,4,256,769]{3,2,1,0:T(8,128)(2,1)} reshape(bf16[3,4,196864]{2,1,0:T(4,128)(2,1)} %slice.24) | data formatting | bytes 9449472 | tf_op jit(solution)/shard_map/while/body/eval_jaxpr/reshape | solution.py:28
  158.9 3.6 fusion.17
  162.5 3.8 multiply_reduce_fusion.2
  172.6 6.8 %tile.18 = bf16[3,4,197376]{2,1,0:T(4,128)(2,1)} reshape(bf16[3,4,257,768]{3,2,1,0:T(8,128)(2,1)} %tile.17) | data formatting | bytes 9474048 | tf_op jit(solution)/shard_map/while/body/eval_jaxpr/tile | solution.py:26
  179.4 6.9 %slice.24 = bf16[3,4,196864]{2,1,0:T(4,128)(2,1)} slice(bf16[3,4,197376]{2,1,0:T(4,128)(2,1)} %tile.18), slice={[0:3], [0:4], [0:196864]} | slice | bytes 9449472 | tf_op jit(solution)/shard_map/while/body/eval_jaxpr/slice | solution.py:27
  186.3 12.9 %reshape.56 = bf16[3,4,256,769]{3,2,1,0:T(8,128)(2,1)} reshape(bf16[3,4,196864]{2,1,0:T(4,128)(2,1)} %slice.24) | data formatting | bytes 9449472 | tf_op jit(solution)/shard_map/while/body/eval_jaxpr/reshape | solution.py:28
  201.0 2.8 copy.24
  203.9 3.6 fusion.17
  207.5 3.8 multiply_reduce_fusion.2
  217.6 6.8 %tile.18 = bf16[3,4,197376]{2,1,0:T(4,128)(2,1)} reshape(bf16[3,4,257,768]{3,2,1,0:T(8,128)(2,1)} %tile.17) | data formatting | bytes 9474048 | tf_op jit(solution)/shard_map/while/body/eval_jaxpr/tile | solution.py:26
  224.4 6.9 %slice.24 = bf16[3,4,196864]{2,1,0:T(4,128)(2,1)} slice(bf16[3,4,197376]{2,1,0:T(4,128)(2,1)} %tile.18), slice={[0:3], [0:4], [0:196864]} | slice | bytes 9449472 | tf_op jit(solution)/shard_map/while/body/eval_jaxpr/slice | solution.py:27
  231.3 12.9 %reshape.56 = bf16[3,4,256,769]{3,2,1,0:T(8,128)(2,1)} reshape(bf16[3,4,196864]{2,1,0:T(4,128)(2,1)} %slice.24) | data formatting | bytes 9449472 | tf_op jit(solution)/shard_map/while/body/eval_jaxpr/reshape | solution.py:28
  246.0 2.8 copy.24
  248.9 3.6 fusion.17
  252.5 3.8 multiply_reduce_fusion.2
  262.6 6.8 %tile.18 = bf16[3,4,197376]{2,1,0:T(4,128)(2,1)} reshape(bf16[3,4,257,768]{3,2,1,0:T(8,128)(2,1)} %tile.17) | data formatting | bytes 9474048 | tf_op jit(solution)/shard_map/while/body/eval_jaxpr/tile | solution.py:26
  269.4 6.9 %slice.24 = bf16[3,4,196864]{2,1,0:T(4,128)(2,1)} slice(bf16[3,4,197376]{2,1,0:T(4,128)(2,1)} %tile.18), slice={[0:3], [0:4], [0:196864]} | slice | bytes 9449472 | tf_op jit(solution)/shard_map/while/body/eval_jaxpr/slice | solution.py:27
  276.3 12.9 %reshape.56 = bf16[3,4,256,769]{3,2,1,0:T(8,128)(2,1)} reshape(bf16[3,4,196864]{2,1,0:T(4,128)(2,1)} %slice.24) | data formatting | bytes 9449472 | tf_op jit(solution)/shard_map/while/body/eval_jaxpr/reshape | solution.py:28
  291.0 2.8 copy.24
  293.9 3.6 fusion.17
  297.5 3.8 multiply_reduce_fusion.2
  307.6 6.8 %tile.18 = bf16[3,4,197376]{2,1,0:T(4,128)(2,1)} reshape(bf16[3,4,257,768]{3,2,1,0:T(8,128)(2,1)} %tile.17) | data formatting | bytes 9474048 | tf_op jit(solution)/shard_map/while/body/eval_jaxpr/tile | solution.py:26
  314.4 6.9 %slice.24 = bf16[3,4,196864]{2,1,0:T(4,128)(2,1)} slice(bf16[3,4,197376]{2,1,0:T(4,128)(2,1)} %tile.18), slice={[0:3], [0:4], [0:196864]} | slice | bytes 9449472 | tf_op jit(solution)/shard_map/while/body/eval_jaxpr/slice | solution.py:27
  321.3 12.9 %reshape.56 = bf16[3,4,256,769]{3,2,1,0:T(8,128)(2,1)} reshape(bf16[3,4,196864]{2,1,0:T(4,128)(2,1)} %slice.24) | data formatting | bytes 9449472 | tf_op jit(solution)/shard_map/while/body/eval_jaxpr/reshape | solution.py:28
  338.9 3.6 fusion.17
  342.5 3.8 multiply_reduce_fusion.2
  352.6 6.8 %tile.18 = bf16[3,4,197376]{2,1,0:T(4,128)(2,1)} reshape(bf16[3,4,257,768]{3,2,1,0:T(8,128)(2,1)} %tile.17) | data formatting | bytes 9474048 | tf_op jit(solution)/shard_map/while/body/eval_jaxpr/tile | solution.py:26
  359.4 6.9 %slice.24 = bf16[3,4,196864]{2,1,0:T(4,128)(2,1)} slice(bf16[3,4,197376]{2,1,0:T(4,128)(2,1)} %tile.18), slice={[0:3], [0:4], [0:196864]} | slice | bytes 9449472 | tf_op jit(solution)/shard_map/while/body/eval_jaxpr/slice | solution.py:27
  366.3 12.9 %reshape.56 = bf16[3,4,256,769]{3,2,1,0:T(8,128)(2,1)} reshape(bf16[3,4,196864]{2,1,0:T(4,128)(2,1)} %slice.24) | data formatting | bytes 9449472 | tf_op jit(solution)/shard_map/while/body/eval_jaxpr/reshape | solution.py:28
  383.9 3.6 fusion.17
  387.5 3.8 multiply_reduce_fusion.2
  395.3 23.3 %reduce-scatter.2.cloned.1.call-done = f32[128,512]{1,0:T(8,128)} async-done(((f32[128,2048]{1,0:T(8,128)}), f32[128,512]{1,0:T(8,128)}) %reduce-scatter.2.cloned.1.call-update) | async-done | bytes 262160 | tf_op jit(solution)/shard_map/reduce_scatter | solution.py:78
  (151 shorter events, 80.0 us)
Async XLA Ops:
  6.5 7.1 %copy-start.3 = (bf16[8,3,512]{2,0,1:T(8,128)(2,1)S(1)}, bf16[8,3,512]{2,0,1:T(8,128)(2,1)}, u32[]{:S(2)}) copy-start(bf16[8,3,512]{2,0,1:T(8,128)(2,1)} %param.9) | copy-start | bytes 73732
  6.5 14.0 %copy-start.2 = (bf16[128,8,3,256]{3,1,2,0:T(8,128)(2,1)S(1)}, bf16[128,8,3,256]{3,1,2,0:T(8,128)(2,1)}, u32[]{:S(2)}) copy-start(bf16[128,8,3,256]{3,1,2,0:T(8,128)(2,1)} %param.8) | copy-start | bytes 4718596
  6.5 7.1 %copy-start.4 = (bf16[8,3,512]{2,0,1:T(8,128)(2,1)S(1)}, bf16[8,3,512]{2,0,1:T(8,128)(2,1)}, u32[]{:S(2)}) copy-start(bf16[8,3,512]{2,0,1:T(8,128)(2,1)} %param.10) | copy-start | bytes 73732
  6.5 15.9 %copy-start.6 = (s32[8]{0:T(128)S(1)}, s32[8]{0:T(128)}, u32[]{:S(2)}) copy-start(s32[8]{0:T(128)} %param.12) | copy-start | bytes 100
  6.5 19.9 %copy-start.5 = (s32[128,8]{0,1:T(8,128)S(1)}, s32[128,8]{0,1:T(8,128)}, u32[]{:S(2)}) copy-start(s32[128,8]{0,1:T(8,128)} %param.13) | copy-start | bytes 12292
  6.5 412.0 %reduce-scatter.2.cloned.1.call-start = ((), (), s32[]{:S(2)}) async-start(), calls=%async_computation.1 | async-start | bytes 1310720 | tf_op jit(solution)/shard_map/reduce_scatter | solution.py:78
  6.6 7.1 %collective-permute-start = (bf16[8,3,512]{2,0,1:T(8,128)(2,1)}, bf16[8,3,512]{2,0,1:T(8,128)(2,1)S(1)}, u32[]{:S(2)}, u32[]{:S(2)}) collective-permute-start(bf16[8,3,512]{2,0,1:T(8,128)(2,1)} %param.9), channel_id=1, source_target_pairs={{4,0},{8,4},{12,8},{5,1},{9,5},{13,9},{6,2},{10,6},{14,10},{7,3},{... | collective-permute-start | bytes 73736 | tf_op jit(solution)/shard_map/ppermute | solution.py:12
  9.9 22.7 %copy-start.7 = (s32[8]{0:T(128)S(1)}, s32[8]{0:T(128)}, u32[]{:S(2)}) copy-start(s32[8]{0:T(128)} %param.11) | copy-start | bytes 100
  13.7 6.9 %collective-permute-start.1 = (bf16[8,3,1024]{2,0,1:T(8,128)(2,1)S(1)}, bf16[8,3,1024]{2,0,1:T(8,128)(2,1)S(1)}, u32[]{:S(2)}, u32[]{:S(2)}) collective-permute-start(bf16[8,3,1024]{2,0,1:T(8,128)(2,1)S(1)} %pad_maximum_fusion), channel_id=1, source_target_pairs={{0,4},{4,8},{8,12},{12,0},{1,5},{5,9},{9,13},{13,1},{2,6},{6,10},{... | collective-permute-start | bytes 147464 | tf_op jit(solution)/shard_map/ppermute | solution.py:55
  20.6 5.9 %collective-permute-start.2 = (bf16[8,3,1024]{2,0,1:T(8,128)(2,1)S(1)}, bf16[8,3,1024]{2,0,1:T(8,128)(2,1)S(1)}, u32[]{:S(2)}, u32[]{:S(2)}) collective-permute-start(bf16[8,3,1024]{2,0,1:T(8,128)(2,1)S(1)} %collective-permute-done.1), channel_id=1, source_target_pairs={{0,4},{4,8},{8,12},{12,0},{1,5},{5,9},{9,13},{13,1},{2,6},{6,10},{... | collective-permute-start | bytes 147464 | tf_op jit(solution)/shard_map/ppermute | solution.py:55
  26.5 5.9 %collective-permute-start.3 = (bf16[8,3,1024]{2,0,1:T(8,128)(2,1)S(1)}, bf16[8,3,1024]{2,0,1:T(8,128)(2,1)S(1)}, u32[]{:S(2)}, u32[]{:S(2)}) collective-permute-start(bf16[8,3,1024]{2,0,1:T(8,128)(2,1)S(1)} %collective-permute-done.2), channel_id=1, source_target_pairs={{0,4},{4,8},{8,12},{12,0},{1,5},{5,9},{9,13},{13,1},{2,6},{6,10},{... | collective-permute-start | bytes 147464 | tf_op jit(solution)/shard_map/ppermute | solution.py:55
  64.2 1.9 slice-start
  72.5 3.8 copy-start
  76.7 1.0 copy-start.1
  109.2 1.9 slice-start
  117.5 3.8 copy-start
  121.7 1.0 copy-start.1
  154.2 1.9 slice-start
  162.5 3.8 copy-start
  166.7 1.0 copy-start.1
  199.2 1.9 slice-start
  207.5 3.8 copy-start
  211.7 1.0 copy-start.1
  244.2 1.9 slice-start
  252.5 3.8 copy-start
  256.7 1.0 copy-start.1
  289.2 1.9 slice-start
  297.5 3.8 copy-start
  301.7 1.0 copy-start.1
  334.2 1.9 slice-start
  342.5 3.8 copy-start
  346.7 1.0 copy-start.1
  379.2 1.9 slice-start
  387.5 3.8 copy-start
  391.7 1.0 copy-start.1
Sparse Core Ops, SparseCore 0:
  395.4 23.0 reduce-scatter.1
